TPU v7x, 256 devices: a whole 4x4x8 slice. The times are simulated.
256 devices in a mesh: tm: 8 (over y, core), head: 32 (over z, x).
Axes of the slice: x: 4, y: 4, z: 8, core: 2. Of those that a mesh axis runs over, the one named last changes fastest.
Arguments:
- tokens: bfloat16 [4096, 5120], P('tm'), may hold values from -24 to 24
- w_query: bfloat16 [5120, 4096], P(None, 'head'), may hold values from -0.078125 to 0.078125
- w_key: bfloat16 [5120, 4096], P(None, 'head'), may hold values from -0.078125 to 0.078125
- w_value: bfloat16 [5120, 4096], P(None, 'head'), may hold values from -0.078125 to 0.078125
- w_out: bfloat16 [4096, 5120], P('head'), may hold values from -0.09375 to 0.09375
- out_grad: bfloat16 [4096, 5120], P('tm'), may hold values from -6 to 6
- frame_lists: int32 [8, 8], replicated, may hold values from 0 to 1, as said below
Outputs:
- token_grad: bfloat16 [4096, 5120], P(('tm', 'head'))
- query_grad: bfloat16 [5120, 4096], P('tm', 'head')
- key_grad: bfloat16 [5120, 4096], P('tm', 'head')
- value_grad: bfloat16 [5120, 4096], P('tm', 'head')
- out_weight_grad: bfloat16 [4096, 5120], P('head', 'tm')
Inputs may be any that keep to these rules, and one draw needn't show every extreme that they name: `frame_lists`: entries with j >= i are 0; entry (i, i - 1) is 1 for every group i > 0.
All inputs are finite; a program needn't handle non-finite values.
Results may differ from a plain program's by a relative error of at most 0.02.
The roundings to bfloat16 on the way count: a program that leaves them out, or rounds other values in their place, can miss the bound.
Values may be sent and summed in bfloat16 or wider, within the bound.
A program may use at most 128 MiB of HBM per device.

v0:
```python
import jax
import jax.numpy as jnp
from jax import lax
from jax.sharding import PartitionSpec as P


def contract_rows(left, right):
    return lax.dot_general(
        left, right, (((0,), (0,)), ((), ())), preferred_element_type=jnp.float32
    )


def contract_cols(left, right):
    return lax.dot_general(
        left, right, (((1,), (1,)), ((), ())), preferred_element_type=jnp.float32
    )


def local(tokens, w_query, w_key, w_value, w_out, out_grad, frame_lists):
    width = w_query.shape[1]
    scale = 1.0 / width**0.5
    rows = tokens.shape[0]
    groups = lax.axis_size("tm")
    mine = lax.axis_index("tm")
    query = jnp.dot(tokens, w_query, preferred_element_type=jnp.float32).astype(jnp.bfloat16)
    keys = jnp.dot(tokens, w_key, preferred_element_type=jnp.float32).astype(jnp.bfloat16)
    values = jnp.dot(tokens, w_value, preferred_element_type=jnp.float32).astype(jnp.bfloat16)
    d_attn = contract_cols(out_grad, w_out).astype(jnp.bfloat16)
    my_list = lax.dynamic_slice_in_dim(frame_lists, mine, 1, 0)[0]
    key_all, value_all = (
        lax.all_gather(keys, "tm", axis=0, tiled=True),
        lax.all_gather(values, "tm", axis=0, tiled=True),
    )
    order = jnp.arange(groups, dtype=jnp.int32)
    allowed = (order == mine) | (my_list == 1) & (order < mine)
    key_mask = jnp.repeat(allowed, rows)[None, :]
    scores = contract_cols(query, key_all) * scale
    scores = jnp.where(key_mask, scores, jnp.float32(-1e30))
    top = jnp.max(scores, axis=1, keepdims=True)
    expd = jnp.exp(scores - top)
    probs = expd / jnp.sum(expd, axis=1, keepdims=True)
    probs_b = probs.astype(jnp.bfloat16)
    attn = jnp.dot(probs_b, value_all, preferred_element_type=jnp.float32).astype(jnp.bfloat16)
    dprobs = contract_cols(d_attn, value_all)
    delta = jnp.sum(probs * dprobs, axis=1, keepdims=True)
    dscore = (probs * (dprobs - delta) * scale).astype(jnp.bfloat16)
    dquery = jnp.dot(dscore, key_all, preferred_element_type=jnp.float32).astype(jnp.bfloat16)
    cache_terms = jnp.concatenate(
        [contract_rows(dscore, query), contract_rows(probs_b, d_attn)], axis=1
    )
    summed = lax.psum_scatter(
        cache_terms.astype(jnp.bfloat16), "tm", scatter_dimension=0, tiled=True
    ).astype(jnp.float32)
    dkey = summed[:, :width].astype(jnp.bfloat16)
    dvalue = summed[:, width:].astype(jnp.bfloat16)
    weights_sum = lax.psum_scatter(
        jnp.concatenate(
            [
                contract_rows(tokens, dquery),
                contract_rows(tokens, dkey),
                contract_rows(tokens, dvalue),
                contract_rows(out_grad, attn),
            ],
            axis=1,
        ).astype(jnp.bfloat16),
        "tm",
        scatter_dimension=0,
        tiled=True,
    ).astype(jnp.float32)
    query_grad = weights_sum[:, :width].astype(jnp.bfloat16)
    key_grad = weights_sum[:, width : 2 * width].astype(jnp.bfloat16)
    value_grad = weights_sum[:, 2 * width : 3 * width].astype(jnp.bfloat16)
    out_weight_grad = weights_sum[:, 3 * width :].T.astype(jnp.bfloat16)
    token_grad = lax.psum_scatter(
        (
            contract_cols(dquery, w_query)
            + contract_cols(dkey, w_key)
            + contract_cols(dvalue, w_value)
        ).astype(jnp.bfloat16),
        "head",
        scatter_dimension=0,
        tiled=True,
    )
    return (token_grad, query_grad, key_grad, value_grad, out_weight_grad)


def solution(mesh):
    in_specs = (
        P("tm", None),
        P(None, "head"),
        P(None, "head"),
        P(None, "head"),
        P("head", None),
        P("tm", None),
        P(),
    )
    out_specs = (
        P(("tm", "head"), None),
        P("tm", "head"),
        P("tm", "head"),
        P("tm", "head"),
        P("head", "tm"),
    )
    return jax.shard_map(local, mesh=mesh, in_specs=in_specs, out_specs=out_specs, check_vma=False)
```

profile of v0, /device:TPU:8, one launch (start us, length us, event | category | flops | bytes accessed | tf_op | source)
XLA Modules:
  0.0 424.9 jit_solution(9849481897770291235)
XLA Ops:
  7.2 5.2 %convolution_convert_fusion.9 = bf16[512,128]{1,0:T(8,128)(2,1)} fusion(bf16[512,5120]{1,0:T(8,128)(2,1)} %param.7, bf16[5120,128]{1,0:T(8,128)(2,1)} %param.9), kind=kOutput, calls=%fused_computation.26 | convolution fusion | flops 671154176 | bytes 6684672 | tf_op jit(solution)/shard_map/dot_general | solution.py:26
  12.5 4.7 %convolution_convert_fusion.7 = bf16[512,128]{1,0:T(8,128)(2,1)} fusion(bf16[512,5120]{1,0:T(8,128)(2,1)} %param.7, bf16[5120,128]{1,0:T(8,128)(2,1)S(1)} %copy-done.7), kind=kOutput, calls=%fused_computation.24 | convolution fusion | flops 671154176 | bytes 6684672 | tf_op jit(solution)/shard_map/dot_general | solution.py:27
  17.3 0.8 fusion.20
  18.1 4.0 convolution_convert_fusion.10
  22.2 4.0 convolution_convert_fusion.8
  26.2 13.5 %all-gather.3.cloned.1.call-done = bf16[4096,128]{1,0:T(8,128)(2,1)} async-done(((bf16[512,128]{1,0:T(8,128)(2,1)}), bf16[4096,128]{1,0:T(8,128)(2,1)}) %all-gather.3.cloned.1.call-update) | async-done | bytes 1048592 | tf_op jit(solution)/shard_map/all_gather | solution.py:31
  39.7 2.7 fusion
  42.5 3.2 copy-done.2
  45.7 2.2 fusion.2
  47.9 20.2 %all-gather.5.cloned.1.call-done = bf16[4096,128]{1,0:T(8,128)(2,1)} async-done(((bf16[512,128]{1,0:T(8,128)(2,1)}), bf16[4096,128]{1,0:T(8,128)(2,1)}) %all-gather.5.cloned.1.call-update) | async-done | bytes 1048592 | tf_op jit(solution)/shard_map/all_gather | solution.py:32
  68.0 7.4 %multiply_reduce_fusion = (f32[512]{0:T(512)S(1)}, f32[512,4096]{1,0:T(8,128)S(1)}, f32[512,4096]{1,0:T(8,128)}) fusion(f32[512]{0:T(512)S(1)} %fusion.2, f32[512]{0:T(512)S(1)} %get-tuple-element.21, f32[512,4096]{1,0:T(8,128)} %copy-done.2, pred[4096]{0:T(1024)(128)(4,1)S(1)} %bitcast.47, bf16[512,128]{1,0:T(8,128)(2,1)S(1)} %convolution_convert_fusion.8, ...), kind=kOutput, calls=%fused_computation.2 | convolution fusion | flops 549453312 | bytes 26355712 | tf_op jit(solution)/shard_map/dot_general | solution.py:14
  75.5 0.8 convolution_convert_fusion.4
  76.2 2.5 copy-done.1
  78.7 8.0 %multiply_convert_fusion = bf16[512,4096]{1,0:T(8,128)(2,1)S(1)} fusion(f32[512,4096]{1,0:T(8,128)} %copy-done.1, f32[512,4096]{1,0:T(8,128)} %get-tuple-element.23, f32[512]{0:T(512)S(1)} %get-tuple-element.15), kind=kLoop, calls=%fused_computation.1 | loop fusion | flops 8388608 | bytes 20973568 | tf_op jit(solution)/shard_map/convert_element_type | solution.py:46
  86.7 2.0 copy-done.3
  88.7 0.8 convolution_convert_fusion.5
  89.5 1.5 pad_maximum_fusion.1
  91.2 3.7 convolution_convert_fusion.6
  94.9 3.4 fusion.3
  98.3 9.7 %fusion.6 = bf16[5120,128]{0,1:T(8,128)(2,1)} fusion(bf16[512,5120]{1,0:T(8,128)(2,1)} %param.12, bf16[4096,128]{1,0:T(8,128)(2,1)} %all-gather.5.cloned.1.call-done, f32[512,4096]{1,0:T(8,128)} %copy-done.1), kind=kOutput, calls=%fused_computation.15 | convolution fusion | flops 1210777600 | bytes 15990784 | tf_op jit(solution)/shard_map/dot_general | solution.py:8
  108.0 17.6 %reduce-scatter.6.cloned.1.call-done = bf16[512,256]{0,1:T(8,128)(2,1)} async-done(((bf16[4096,256]{0,1:T(8,128)(2,1)}), bf16[512,256]{0,1:T(8,128)(2,1)}) %reduce-scatter.6.cloned.1.call-update) | async-done | bytes 262160 | tf_op jit(solution)/shard_map/reduce_scatter | solution.py:51
  125.6 3.5 fusion.4
  129.1 3.4 fusion.5
  132.6 3.5 pad_maximum_fusion
  136.1 7.9 %copy.18 = bf16[5120,512]{1,0:T(8,128)(2,1)} copy(bf16[5120,512]{0,1:T(8,128)(2,1)} %pad_maximum_fusion) | data formatting | bytes 10485760
  144.1 1.5 fusion.23
  145.6 5.5 %fusion.18 = f32[512,5120]{1,0:T(8,128)} fusion(bf16[5120,128]{1,0:T(8,128)(2,1)S(1)} %copy-done.6, bf16[512,256]{0,1:T(8,128)(2,1)S(1)} %copy-done.5), kind=kOutput, calls=%fused_computation.32 | convolution fusion | flops 671088640 | bytes 11927552 | tf_op jit(solution)/shard_map/dot_general | solution.py:14
  151.2 8.2 %add_convert_fusion = bf16[512,5120]{1,0:T(8,128)(2,1)} fusion(f32[512,5120]{1,0:T(8,128)S(1)} %fusion.23, f32[512,5120]{1,0:T(8,128)} %fusion.18, bf16[5120,128]{1,0:T(8,128)(2,1)S(1)} %copy-done.8, bf16[512,256]{0,1:T(8,128)(2,1)S(1)} %copy-done.5), kind=kOutput, calls=%fused_computation | convolution fusion | flops 678952960 | bytes 27656192 | tf_op jit(solution)/shard_map/dot_general | solution.py:14
  159.4 25.7 %reduce-scatter.10.cloned.1.call-done = bf16[640,512]{1,0:T(8,128)(2,1)} async-done(((bf16[5120,512]{1,0:T(8,128)(2,1)}), bf16[640,512]{1,0:T(8,128)(2,1)}) %reduce-scatter.10.cloned.1.call-update) | async-done | bytes 655376
  185.1 2.0 fusion.22
  187.0 0.8 copy.23
  187.8 230.5 %reduce-scatter.8.cloned.1.call-done = bf16[16,5120]{1,0:T(8,128)(2,1)} async-done(((bf16[512,5120]{1,0:T(8,128)(2,1)}), bf16[16,5120]{1,0:T(8,128)(2,1)}) %reduce-scatter.8.cloned.1.call-update) | async-done | bytes 163856 | tf_op jit(solution)/shard_map/reduce_scatter | solution.py:74
  (29 shorter events, 0.6 us)
Async XLA Ops:
  7.2 11.0 %copy-start = (bf16[5120,128]{1,0:T(8,128)(2,1)S(1)}, bf16[5120,128]{1,0:T(8,128)(2,1)}, u32[]{:S(2)}) copy-start(bf16[5120,128]{1,0:T(8,128)(2,1)} %param.8) | copy-start | bytes 3932164
  7.2 5.3 %copy-start.7 = (bf16[5120,128]{1,0:T(8,128)(2,1)S(1)}, bf16[5120,128]{1,0:T(8,128)(2,1)}, u32[]{:S(2)}) copy-start(bf16[5120,128]{1,0:T(8,128)(2,1)} %param.10) | copy-start | bytes 3932164
  7.2 32.6 %all-gather.3.cloned.1.call-start = ((), (), s32[]{:S(2)}) async-start(), calls=%async_computation.3 | async-start | bytes 1179648 | tf_op jit(solution)/shard_map/all_gather | solution.py:31
  12.5 55.6 %all-gather.5.cloned.1.call-start = ((), (), s32[]{:S(2)}) async-start(), calls=%async_computation.4 | async-start | bytes 1179648 | tf_op jit(solution)/shard_map/all_gather | solution.py:32
  17.2 5.0 %copy-start.9 = (bf16[128,5120]{1,0:T(8,128)(2,1)S(1)}, bf16[128,5120]{1,0:T(8,128)(2,1)}, u32[]{:S(2)}) copy-start(bf16[128,5120]{1,0:T(8,128)(2,1)} %param.11) | copy-start | bytes 3932164
  17.2 108.4 %reduce-scatter.6.cloned.1.call-start = ((), (), s32[]{:S(2)}) async-start(), calls=%async_computation.5 | async-start | bytes 2359296 | tf_op jit(solution)/shard_map/reduce_scatter | solution.py:51
  42.5 3.2 copy-start.2
  75.4 3.2 copy-start.1
  86.7 2.0 copy-start.3
  91.0 94.1 %reduce-scatter.10.cloned.1.call-start = ((), (), s32[]{:S(2)}) async-start(), calls=%async_computation.7 | async-start | bytes 5898240
  125.6 3.5 copy-start.5
  129.1 3.5 copy-start.4
  144.0 1.6 copy-start.6
  144.0 274.3 %reduce-scatter.8.cloned.1.call-start = ((), (), s32[]{:S(2)}) async-start(), calls=%async_computation.6 | async-start | bytes 5406720 | tf_op jit(solution)/shard_map/reduce_scatter | solution.py:74
  145.6 5.5 %copy-start.8 = (bf16[5120,128]{1,0:T(8,128)(2,1)S(1)}, bf16[5120,128]{1,0:T(8,128)(2,1)}, u32[]{:S(2)}) copy-start(bf16[5120,128]{1,0:T(8,128)(2,1)} %param.10) | copy-start | bytes 3932164
Sparse Core Ops, SparseCore 0:
  12.6 27.1 all-gather.2
  42.2 25.7 all-gather.4
  91.1 34.4 reduce-scatter.5
  144.1 40.9 reduce-scatter.9
  189.5 228.8 reduce-scatter.7
where the time goes:
time: 425 us
  waiting for transfers between devices  308 us (72%)
  matrix products  68.5 us (16%)
  local copies, waits for them, and re-layouts  18.5 us (4%)
  other arithmetic  16 us (4%)
  between operations  14 us (3%)
    reduce_scatter x1, waiting for transfers between devices, local(): lax.psum_scatter((contract_cols(dquery, w_query) + contract_cols(dkey, w_...  231 us
    dot_general x6, matrix products, contract_cols(): lax.dot_general(left, right, (((1,), (1,)), ((), ())), preferred_element_...  29.4 us
    unnamed x6, waiting for transfers between devices  25.8 us
    dot_general x6, matrix products, contract_rows(): lax.dot_general(left, right, (((0,), (0,)), ((), ())), preferred_element_...  21.5 us
    all_gather x1, waiting for transfers between devices, local(): lax.all_gather(values, 'tm', axis=0, tiled=True)  20.2 us
    reduce_scatter x1, waiting for transfers between devices, local(): lax.psum_scatter(cache_terms.astype(jnp.bfloat16), 'tm', scatter_dimensio...  17.6 us
    unnamed x24, local copies, waits for them, and re-layouts  16.5 us
    all_gather x1, waiting for transfers between devices, local(): lax.all_gather(keys, 'tm', axis=0, tiled=True)  13.5 us
  transfers between devices with their start and end apart: 5, of which 5 were waited for; matrix products, arithmetic and copies ran while one was open for 13% of the time, Pallas kernels for 0%

commit v1 on v0

--- a/solution.py
+++ b/solution.py
@@ -29,7 +29,9 @@
     my_list = lax.dynamic_slice_in_dim(frame_lists, mine, 1, 0)[0]
     key_all, value_all = (
         lax.all_gather(keys, "tm", axis=0, tiled=True),
-        lax.all_gather(values, "tm", axis=0, tiled=True),
+        jnp.concatenate(
+            lax.all_to_all(jnp.stack([values] * lax.axis_size("tm")), "tm", 0, 0), axis=0
+        ),
     )
     order = jnp.arange(groups, dtype=jnp.int32)
     allowed = (order == mine) | (my_list == 1) & (order < mine)

time: 425 us -> 408 us (0.960)
  waiting for transfers between devices: 308 us -> 284 us
  starting transfers between devices: 0.39 us -> 6 us
    all_gather x1 -> x0, waiting for transfers between devices: 20.2 us -> none  [local(): lax.all_gather(values, 'tm', axis=0, tiled=True)]
    all_to_all x0 -> x1, starting transfers between devices: none -> 5.65 us  [local(): lax.all_to_all(jnp.stack([values] * lax.axis_size('tm')), 'tm', 0, 0)]
    unnamed x24 -> x28, local copies, waits for them, and re-layouts: 16.5 us -> 15.5 us
    unnamed x6 -> x5, waiting for transfers between devices: 25.8 us -> 25.8 us
  transfers between devices with their start and end apart: 5 -> 5, of which waited for: 5 -> 4; matrix products, arithmetic and copies ran while one was open for 13% -> 13% of each run, Pallas kernels for 0% -> 0%
where the time goes in v1:
time: 408 us; the launch traced here: 407 us
  waiting for transfers between devices  284 us (70%)
  matrix products  69 us (17%)
  local copies, waits for them, and re-layouts  18.6 us (5%)
  other arithmetic  16 us (4%)
  between operations  14 us (3%)
  starting transfers between devices  6 us (1%)
    reduce_scatter x1, waiting for transfers between devices, local(): lax.psum_scatter((contract_cols(dquery, w_query) + contract_cols(dkey, w_...  230 us
    dot_general x6, matrix products, contract_cols(): lax.dot_general(left, right, (((1,), (1,)), ((), ())), preferred_element_...  29.5 us
    unnamed x5, waiting for transfers between devices  25.8 us
    dot_general x6, matrix products, contract_rows(): lax.dot_general(left, right, (((0,), (0,)), ((), ())), preferred_element_...  22.5 us
    reduce_scatter x1, waiting for transfers between devices, local(): lax.psum_scatter(cache_terms.astype(jnp.bfloat16), 'tm', scatter_dimensio...  16.9 us
    unnamed x28, local copies, waits for them, and re-layouts  15.5 us
    all_gather x1, waiting for transfers between devices, local(): lax.all_gather(keys, 'tm', axis=0, tiled=True)  10.6 us
  transfers between devices with their start and end apart: 5, of which 4 were waited for; matrix products, arithmetic and copies ran while one was open for 13% of the time, Pallas kernels for 0%

profile of v1, /device:TPU:8, one launch (start us, length us, event | category | flops | bytes accessed | tf_op | source)
XLA Modules:
  0.0 407.3 jit_solution(5775423381515940925)
XLA Ops:
  7.2 5.2 %convolution_convert_fusion.9 = bf16[512,128]{1,0:T(8,128)(2,1)} fusion(bf16[512,5120]{1,0:T(8,128)(2,1)} %param.7, bf16[5120,128]{1,0:T(8,128)(2,1)} %param.9), kind=kOutput, calls=%fused_computation.26 | convolution fusion | flops 671154176 | bytes 6684672 | tf_op jit(solution)/shard_map/dot_general | solution.py:26
  12.5 4.0 convolution_convert_fusion.7
  16.5 1.2 stack.2
  17.7 5.7 %all-to-all-start = ((bf16[8,512,128]{2,1,0:T(8,128)(2,1)}), bf16[8,512,128]{2,1,0:T(8,128)(2,1)S(1)}, u32[]{:S(2)}, u32[]{:S(2)}) async-start(bf16[8,512,128]{2,1,0:T(8,128)(2,1)} %stack.2), calls=%async_computation | async-start | bytes 2097152 | tf_op jit(solution)/shard_map/all_to_all | solution.py:33
  23.3 0.8 fusion.20
  24.2 4.0 convolution_convert_fusion.10
  28.3 4.0 convolution_convert_fusion.8
  32.3 10.6 %all-gather.2.cloned.1.call-done = bf16[4096,128]{1,0:T(8,128)(2,1)} async-done(((bf16[512,128]{1,0:T(8,128)(2,1)}), bf16[4096,128]{1,0:T(8,128)(2,1)}) %all-gather.2.cloned.1.call-update) | async-done | bytes 1048592 | tf_op jit(solution)/shard_map/all_gather | solution.py:31
  42.9 2.7 fusion
  45.6 3.2 copy-done.2
  48.8 2.2 fusion.2
  51.0 7.5 %multiply_reduce_fusion = (f32[512]{0:T(512)S(1)}, f32[512,4096]{1,0:T(8,128)S(1)}, f32[512,4096]{1,0:T(8,128)}) fusion(f32[512]{0:T(512)S(1)} %fusion.2, f32[512]{0:T(512)S(1)} %get-tuple-element.21, f32[512,4096]{1,0:T(8,128)} %copy-done.2, pred[4096]{0:T(1024)(128)(4,1)S(1)} %bitcast.50, bf16[512,128]{1,0:T(8,128)(2,1)S(1)} %convolution_convert_fusion.8, ...), kind=kOutput, calls=%fused_computation.2 | convolution fusion | flops 549453312 | bytes 26355712 | tf_op jit(solution)/shard_map/dot_general | solution.py:14
  58.6 1.8 convolution_convert_fusion.4
  60.3 1.4 copy-done.1
  61.8 8.0 %multiply_convert_fusion = bf16[512,4096]{1,0:T(8,128)(2,1)S(1)} fusion(f32[512,4096]{1,0:T(8,128)} %copy-done.1, f32[512,4096]{1,0:T(8,128)} %get-tuple-element.23, f32[512]{0:T(512)S(1)} %get-tuple-element.15), kind=kLoop, calls=%fused_computation.1 | loop fusion | flops 8388608 | bytes 20973568 | tf_op jit(solution)/shard_map/convert_element_type | solution.py:48
  69.8 2.0 copy-done.3
  72.6 1.5 pad_maximum_fusion.1
  74.3 3.7 convolution_convert_fusion.6
  78.1 3.4 fusion.3
  81.5 9.7 %fusion.6 = bf16[5120,128]{0,1:T(8,128)(2,1)} fusion(bf16[512,5120]{1,0:T(8,128)(2,1)} %param.12, bf16[4096,128]{1,0:T(8,128)(2,1)} %bitcast.46, f32[512,4096]{1,0:T(8,128)} %copy-done.1), kind=kOutput, calls=%fused_computation.15 | convolution fusion | flops 1210777600 | bytes 15990784 | tf_op jit(solution)/shard_map/dot_general | solution.py:8
  91.2 16.9 %reduce-scatter.6.cloned.1.call-done = bf16[512,256]{0,1:T(8,128)(2,1)} async-done(((bf16[4096,256]{0,1:T(8,128)(2,1)}), bf16[512,256]{0,1:T(8,128)(2,1)}) %reduce-scatter.6.cloned.1.call-update) | async-done | bytes 262160 | tf_op jit(solution)/shard_map/reduce_scatter | solution.py:53
  108.1 3.4 fusion.4
  111.6 3.4 fusion.5
  115.1 3.5 pad_maximum_fusion
  118.6 7.9 %copy.18 = bf16[5120,512]{1,0:T(8,128)(2,1)} copy(bf16[5120,512]{0,1:T(8,128)(2,1)} %pad_maximum_fusion) | data formatting | bytes 10485760
  126.6 1.5 fusion.23
  128.2 5.5 %fusion.18 = f32[512,5120]{1,0:T(8,128)} fusion(bf16[5120,128]{1,0:T(8,128)(2,1)S(1)} %copy-done.7, bf16[512,256]{0,1:T(8,128)(2,1)S(1)} %copy-done.6), kind=kOutput, calls=%fused_computation.32 | convolution fusion | flops 671088640 | bytes 11927552 | tf_op jit(solution)/shard_map/dot_general | solution.py:14
  133.7 8.2 %add_convert_fusion = bf16[512,5120]{1,0:T(8,128)(2,1)} fusion(f32[512,5120]{1,0:T(8,128)S(1)} %fusion.23, f32[512,5120]{1,0:T(8,128)} %fusion.18, bf16[5120,128]{1,0:T(8,128)(2,1)S(1)} %copy-done.9, bf16[512,256]{0,1:T(8,128)(2,1)S(1)} %copy-done.6), kind=kOutput, calls=%fused_computation | convolution fusion | flops 678952960 | bytes 27656192 | tf_op jit(solution)/shard_map/dot_general | solution.py:14
  141.9 25.8 %reduce-scatter.10.cloned.1.call-done = bf16[640,512]{1,0:T(8,128)(2,1)} async-done(((bf16[5120,512]{1,0:T(8,128)(2,1)}), bf16[640,512]{1,0:T(8,128)(2,1)}) %reduce-scatter.10.cloned.1.call-update) | async-done | bytes 655376
  167.7 2.0 fusion.22
  169.6 0.8 copy.23
  170.4 230.4 %reduce-scatter.8.cloned.1.call-done = bf16[16,5120]{1,0:T(8,128)(2,1)} async-done(((bf16[512,5120]{1,0:T(8,128)(2,1)}), bf16[16,5120]{1,0:T(8,128)(2,1)}) %reduce-scatter.8.cloned.1.call-update) | async-done | bytes 163856 | tf_op jit(solution)/shard_map/reduce_scatter | solution.py:76
  (33 shorter events, 1.3 us)
Async XLA Ops:
  7.2 17.1 %copy-start = (bf16[5120,128]{1,0:T(8,128)(2,1)S(1)}, bf16[5120,128]{1,0:T(8,128)(2,1)}, u32[]{:S(2)}) copy-start(bf16[5120,128]{1,0:T(8,128)(2,1)} %param.8) | copy-start | bytes 3932164
  7.2 5.3 %copy-start.8 = (bf16[5120,128]{1,0:T(8,128)(2,1)S(1)}, bf16[5120,128]{1,0:T(8,128)(2,1)}, u32[]{:S(2)}) copy-start(bf16[5120,128]{1,0:T(8,128)(2,1)} %param.10) | copy-start | bytes 3932164
  7.2 35.7 %all-gather.2.cloned.1.call-start = ((), (), s32[]{:S(2)}) async-start(), calls=%async_computation.4 | async-start | bytes 1179648 | tf_op jit(solution)/shard_map/all_gather | solution.py:31
  17.7 33.3 %all-to-all-start = ((bf16[8,512,128]{2,1,0:T(8,128)(2,1)}), bf16[8,512,128]{2,1,0:T(8,128)(2,1)S(1)}, u32[]{:S(2)}, u32[]{:S(2)}) async-start(bf16[8,512,128]{2,1,0:T(8,128)(2,1)} %stack.2), calls=%async_computation | async-start | bytes 2097152 | tf_op jit(solution)/shard_map/all_to_all | solution.py:33
  23.3 84.8 %reduce-scatter.6.cloned.1.call-start = ((), (), s32[]{:S(2)}) async-start(), calls=%async_computation.5 | async-start | bytes 2359296 | tf_op jit(solution)/shard_map/reduce_scatter | solution.py:53
  23.3 4.9 %copy-start.11 = (bf16[128,5120]{1,0:T(8,128)(2,1)S(1)}, bf16[128,5120]{1,0:T(8,128)(2,1)}, u32[]{:S(2)}) copy-start(bf16[128,5120]{1,0:T(8,128)(2,1)} %param.11) | copy-start | bytes 3932164
  32.3 18.7 %copy-start.10 = (bf16[512,128]{1,0:T(8,128)(2,1)}, bf16[512,128]{1,0:T(8,128)(2,1)S(1)}, u32[]{:S(2)}) copy-start(bf16[512,128]{1,0:T(8,128)(2,1)S(1)} %convolution_convert_fusion.8) | copy-start | bytes 393220
  45.6 3.2 copy-start.2
  51.0 7.5 %copy-start.5 = (bf16[8,512,128]{2,1,0:T(8,128)(2,1)}, bf16[8,512,128]{2,1,0:T(8,128)(2,1)S(1)}, u32[]{:S(2)}) copy-start(bf16[8,512,128]{2,1,0:T(8,128)(2,1)S(1)} %all-to-all-done) | copy-start | bytes 3145732
  58.6 3.2 copy-start.1
  69.8 2.0 copy-start.3
  74.1 93.6 %reduce-scatter.10.cloned.1.call-start = ((), (), s32[]{:S(2)}) async-start(), calls=%async_computation.7 | async-start | bytes 5898240
  108.1 3.5 copy-start.6
  111.6 3.5 copy-start.4
  126.5 1.6 copy-start.7
  126.5 274.3 %reduce-scatter.8.cloned.1.call-start = ((), (), s32[]{:S(2)}) async-start(), calls=%async_computation.6 | async-start | bytes 5406720 | tf_op jit(solution)/shard_map/reduce_scatter | solution.py:76
  128.1 5.6 %copy-start.9 = (bf16[5120,128]{1,0:T(8,128)(2,1)S(1)}, bf16[5120,128]{1,0:T(8,128)(2,1)}, u32[]{:S(2)}) copy-start(bf16[5120,128]{1,0:T(8,128)(2,1)} %param.10) | copy-start | bytes 3932164
Sparse Core Ops, SparseCore 0:
  12.6 30.2 all-gather.1
  74.2 33.8 reduce-scatter.5
  126.7 40.9 reduce-scatter.9
  172.0 228.7 reduce-scatter.7
